TPU v7x, 32 devices: a whole 2x2x4 slice. The times are simulated.
32 devices in a mesh: section: 2 (over x), dp: 4 (over y, core), tensor: 4 (over z).
Axes of the slice: x: 2, y: 2, z: 4, core: 2. Of those that a mesh axis runs over, the one named last changes fastest.
Arguments:
- inputs: bfloat16 [8, 1024, 1024], P('dp', 'tensor'), may hold values from -6 to 6
- out_cotangent: bfloat16 [8, 1024, 1024], P('dp', 'tensor'), may hold values from -6 to 6
- group_ids: int32 [8, 1024], P('dp', 'tensor'), may hold values from 0 to 7
- group_weights: float32 [8], replicated, may hold values from 0.25 to 4
- gains: float32 [2, 4, 1024], P('section'), may hold values from 0.1 to 1.9
- qkv_weight: bfloat16 [2, 1024, 3, 1024], P('section', None, None, 'tensor'), may hold values from -0.1875 to 0.1875
- out_weight: bfloat16 [2, 1024, 1024], P('section', 'tensor'), may hold values from -0.1875 to 0.1875
- up_weight: bfloat16 [2, 1024, 4096], P('section', None, 'tensor'), may hold values from -0.1875 to 0.1875
- down_weight: bfloat16 [2, 4096, 1024], P('section', 'tensor'), may hold values from -0.09375 to 0.09375
Outputs:
- layer_outputs: bfloat16 [2, 8, 1024, 1024], P('section', 'dp', 'tensor')
- input_grads: bfloat16 [2, 8, 1024, 1024], P('section', 'dp', 'tensor')
- gains_grad: float32 [2, 4, 1024], P('section', None, ('dp', 'tensor'))
- qkv_grad: float32 [2, 1024, 3, 1024], P('section', 'dp', None, 'tensor')
- out_grad: float32 [2, 1024, 1024], P('section', 'tensor', 'dp')
- up_grad: float32 [2, 1024, 4096], P('section', 'dp', 'tensor')
- down_grad: float32 [2, 4096, 1024], P('section', 'tensor', 'dp')
All inputs are finite; a program needn't handle non-finite values.
Results may differ from a plain program's by a relative error of at most 0.02.
Values may be sent and summed in bfloat16 or wider, within the bound.
No kernel may reach another device: no remote copies, remote signals or barrier semaphores. Data moves between devices by JAX's collectives and lax.ppermute only.
A program may use at most 192 MiB of HBM per device.

v0:
```python
import jax
import jax.numpy as jnp
from jax import lax
from jax.sharding import PartitionSpec as P

HEAD_DIM = 64
NORM_EPSILON = 1e-06


def shifted(block, axis, distance):
    devices = range(lax.axis_size(axis))
    route = [(i - distance, i) for i in devices if i - distance in devices]
    return lax.ppermute(block, axis, route)


def norm_rows(vector, weight_gain):
    return (
        vector
        * lax.rsqrt(jnp.mean(vector * vector, axis=-1, keepdims=True) + NORM_EPSILON)
        * weight_gain
    )


def rotary_tables(seq_len, head_width):
    half_width = head_width // 2
    freqs = 10000.0 ** (-2.0 * jnp.arange(half_width, dtype=jnp.float32) / head_width)
    angles = jnp.arange(seq_len, dtype=jnp.float32)[:, None] * freqs[None, :]
    return (jnp.cos(angles), jnp.sin(angles))


def rotate(vector, cos_table, sin_table):
    first_half, second_half = jnp.split(vector, 2, axis=-1)
    cos_part = cos_table[:, None, :]
    sin_part = sin_table[:, None, :]
    return jnp.concatenate(
        [
            first_half * cos_part - second_half * sin_part,
            second_half * cos_part + first_half * sin_part,
        ],
        axis=-1,
    )


def contract(left_rows, right_rows):
    return lax.dot_general(
        left_rows, right_rows, (((0,), (0,)), ((), ())), preferred_element_type=jnp.float32
    )


def gather_rows(row_values, weight):

    def project(shard_rows, offset):
        return (shard_rows, jnp.dot(shard_rows, weight, preferred_element_type=jnp.float32))

    return project(lax.all_gather(row_values, "tensor", axis=0, tiled=True), jnp.int32(0))


def scatter_rows(row_values, weight, row_count):

    def partial_term(offset, span):
        return jnp.dot(row_values, weight, preferred_element_type=jnp.float32)

    return lax.psum_scatter(
        partial_term(jnp.int32(0), lax.axis_size("tensor") * row_count),
        "tensor",
        scatter_dimension=0,
        tiled=True,
    )


def gather_grads(row_values, weight):

    def project(shard_rows, offset):
        return (shard_rows, jnp.dot(shard_rows, weight.T, preferred_element_type=jnp.float32))

    return project(lax.all_gather(row_values, "tensor", axis=0, tiled=True), jnp.int32(0))


def scatter_grads(row_values, weight, row_count):

    def partial_term(offset, span):
        return jnp.dot(row_values, weight.T, preferred_element_type=jnp.float32)

    return lax.psum_scatter(
        partial_term(jnp.int32(0), lax.axis_size("tensor") * row_count),
        "tensor",
        scatter_dimension=0,
        tiled=True,
    )


def attention_probs(queries, key_rows):
    scores = jnp.einsum(
        "qhd,khd->hqk", queries, key_rows, preferred_element_type=jnp.float32
    ) * HEAD_DIM ** (-0.5)
    length = queries.shape[0]
    positions = jnp.arange(length, dtype=jnp.int32)
    causal = positions[:, None] >= positions[None, :]
    scores = jnp.where(causal[None], scores, -1e30)
    expos = jnp.exp(scores - jnp.max(scores, axis=-1, keepdims=True))
    return expos / jnp.sum(expos, axis=-1, keepdims=True)


def layer_forward(layer_input, weights):
    gains, w_qkv, w_out, w_up, w_down = weights
    row_count, model_width = layer_input.shape
    attn_in = norm_rows(layer_input, gains[0]).astype(jnp.bfloat16)
    gathered_a, qkv = gather_rows(attn_in, w_qkv.reshape(model_width, -1))
    length = qkv.shape[0]
    head_count = w_qkv.shape[2] // HEAD_DIM
    qkv = qkv.reshape(length, 3, head_count, HEAD_DIM)
    cos_table, sin_table = rotary_tables(length, HEAD_DIM)
    queries = rotate(qkv[:, 0], cos_table, sin_table).astype(jnp.bfloat16)
    key_rows = rotate(qkv[:, 1], cos_table, sin_table).astype(jnp.bfloat16)
    values = qkv[:, 2].astype(jnp.bfloat16)
    attn_probs = attention_probs(queries, key_rows).astype(jnp.bfloat16)
    mixed = jnp.einsum("hqk,khd->qhd", attn_probs, values, preferred_element_type=jnp.float32)
    mixed = mixed.reshape(length, -1).astype(jnp.bfloat16)
    attn_branch = scatter_rows(mixed, w_out, row_count)
    hidden = layer_input + norm_rows(attn_branch, gains[1])
    mlp_in = norm_rows(hidden, gains[2]).astype(jnp.bfloat16)
    gathered_c, up_act = gather_rows(mlp_in, w_up)
    gelu_out = jax.nn.gelu(up_act, approximate=True).astype(jnp.bfloat16)
    down_branch = scatter_rows(gelu_out, w_down, row_count)
    result = hidden + norm_rows(down_branch, gains[3])
    kept_values = (
        gathered_a,
        queries,
        key_rows,
        values,
        mixed,
        attn_branch,
        hidden,
        gathered_c,
        up_act,
        gelu_out,
        down_branch,
    )
    return (result, kept_values)


def layer_backward(layer_input, grad_result, kept_values, weights):
    gains, w_qkv, w_out, w_up, w_down = weights
    (
        gathered_a,
        queries,
        key_rows,
        values,
        mixed,
        attn_branch,
        hidden,
        gathered_c,
        up_act,
        gelu_out,
        down_branch,
    ) = kept_values
    row_count, model_width = layer_input.shape
    pullback = jax.vjp(norm_rows, down_branch, gains[3])[1]
    grad_down, gain_three = pullback(grad_result)
    gathered_dd, grad_gelu = gather_grads(grad_down.astype(jnp.bfloat16), w_down)
    down_total = contract(gelu_out, gathered_dd)
    pullback = jax.vjp(lambda vector: jax.nn.gelu(vector, approximate=True), up_act)[1]
    grad_up = pullback(grad_gelu)[0].astype(jnp.bfloat16)
    up_total = contract(gathered_c, grad_up)
    grad_mlp = scatter_grads(grad_up, w_up, row_count)
    pullback = jax.vjp(norm_rows, hidden, gains[2])[1]
    grad_norm_mlp, gain_two = pullback(grad_mlp)
    grad_hidden = grad_result + grad_norm_mlp
    pullback = jax.vjp(norm_rows, attn_branch, gains[1])[1]
    grad_attn, gain_one = pullback(grad_hidden)
    gathered_da, grad_mixed = gather_grads(grad_attn.astype(jnp.bfloat16), w_out)
    out_total = contract(mixed, gathered_da)
    length = grad_mixed.shape[0]
    head_count = w_qkv.shape[2] // HEAD_DIM
    grad_mixed = grad_mixed.astype(jnp.bfloat16).reshape(length, head_count, HEAD_DIM)
    attn_probs = attention_probs(queries, key_rows)
    probs_low = attn_probs.astype(jnp.bfloat16)
    grad_probs = jnp.einsum("qhd,khd->hqk", grad_mixed, values, preferred_element_type=jnp.float32)
    grad_values = jnp.einsum(
        "hqk,qhd->khd", probs_low, grad_mixed, preferred_element_type=jnp.float32
    )
    row_dots = jnp.sum(grad_probs * attn_probs, axis=-1, keepdims=True)
    grad_scores = (attn_probs * (grad_probs - row_dots)).astype(jnp.bfloat16)
    scale_value = HEAD_DIM ** (-0.5)
    grad_queries = (
        jnp.einsum("hqk,khd->qhd", grad_scores, key_rows, preferred_element_type=jnp.float32)
        * scale_value
    )
    grad_keys = (
        jnp.einsum("hqk,qhd->khd", grad_scores, queries, preferred_element_type=jnp.float32)
        * scale_value
    )
    cos_table, sin_table = rotary_tables(length, HEAD_DIM)
    pullback = jax.vjp(lambda vector: rotate(vector, cos_table, sin_table), grad_queries)[1]
    grad_q_raw = pullback(grad_queries)[0]
    grad_k_raw = pullback(grad_keys)[0]
    grad_qkv = (
        jnp.stack([grad_q_raw, grad_k_raw, grad_values], axis=1)
        .reshape(length, -1)
        .astype(jnp.bfloat16)
    )
    qkv_total = contract(gathered_a, grad_qkv).reshape(model_width, 3, -1)
    grad_attn_in = scatter_grads(grad_qkv, w_qkv.reshape(model_width, -1), row_count)
    pullback = jax.vjp(norm_rows, layer_input, gains[0])[1]
    grad_norm_in, gain_zero = pullback(grad_attn_in)
    grad_input = grad_hidden + grad_norm_in
    gain_total = jnp.stack([gain_zero, gain_one, gain_two, gain_three])
    return (grad_input, (gain_total, qkv_total, out_total, up_total, down_total))


def lagged(first_section, stacked):
    blank = jnp.zeros_like(stacked[:1])
    earlier = jnp.concatenate([blank, stacked[:-1]])
    later = jnp.concatenate([stacked[1:], blank])
    return jnp.where(first_section, earlier, later)


def per_device(
    inputs,
    out_cotangent,
    group_ids,
    group_weights,
    gains,
    qkv_weight,
    out_weight,
    up_weight,
    down_weight,
):
    weights = (gains[0], qkv_weight[0], out_weight[0], up_weight[0], down_weight[0])
    micro_count, row_count, model_width = inputs.shape
    first_section = lax.axis_index("section") == 0
    group_count = group_weights.shape[0]
    matches = group_ids[..., None] == jnp.arange(group_count, dtype=jnp.int32)
    row_scale = jnp.sum(jnp.where(matches, group_weights, 0.0), axis=-1)
    scaled = out_cotangent.astype(jnp.float32) * row_scale[..., None]
    padded = jnp.concatenate([inputs, jnp.zeros((1, row_count, model_width), jnp.bfloat16)])

    def forward_tick(received, fresh_input):
        layer_input = jnp.where(first_section, fresh_input, received)
        result, kept_values = layer_forward(layer_input.astype(jnp.float32), weights)
        result_low = result.astype(jnp.bfloat16)
        outgoing = shifted(result_low, "section", 1)
        stashed = ()
        return (outgoing, (layer_input, result_low, stashed))

    start_rows = jnp.zeros((row_count, model_width), jnp.bfloat16)
    _, (layer_inputs, layer_results, stashed) = lax.scan(forward_tick, start_rows, padded)
    layer_outputs = jnp.where(first_section, layer_results[:-1], layer_results[1:])[None]
    back_inputs = lagged(first_section, layer_inputs)
    back_stash = jax.tree.map(lambda stacked: lagged(first_section, stacked), stashed)
    grad_padded = jnp.concatenate([scaled, jnp.zeros((1, row_count, model_width), jnp.float32)])
    tick_index = jnp.arange(micro_count + 1, dtype=jnp.int32)
    tick_valid = jnp.where(first_section, tick_index >= 1, tick_index < micro_count).astype(
        jnp.float32
    )

    def backward_tick(carry, step_item):
        received, totals = carry
        layer_input, cotangent, valid_now, stash_now = step_item
        grad_now = jnp.where(first_section, received.astype(jnp.float32), cotangent)
        input_now = layer_input.astype(jnp.float32)
        kept_values = layer_forward(input_now, weights)[1]
        grad_input, layer_grads = layer_backward(input_now, grad_now, kept_values, weights)
        totals = jax.tree.map(lambda total, update: total + valid_now * update, totals, layer_grads)
        grad_low = grad_input.astype(jnp.bfloat16)
        outgoing = shifted(grad_low, "section", -1)
        return ((outgoing, totals), grad_low)

    start_totals = (
        jnp.zeros((4, model_width), jnp.float32),
        jnp.zeros(qkv_weight.shape[1:], jnp.float32),
        jnp.zeros(out_weight.shape[1:], jnp.float32),
        jnp.zeros(up_weight.shape[1:], jnp.float32),
        jnp.zeros(down_weight.shape[1:], jnp.float32),
    )
    (_, totals), grad_lows = lax.scan(
        backward_tick,
        (start_rows, start_totals),
        (back_inputs, grad_padded, tick_valid, back_stash),
    )
    input_grads = jnp.where(first_section, grad_lows[1:], grad_lows[:-1])[None]
    gain_total, qkv_total, out_total, up_total, down_total = totals
    gains_grad = lax.psum_scatter(gain_total, ("dp", "tensor"), scatter_dimension=1, tiled=True)
    qkv_grad, out_grad, up_grad, down_grad = (
        lax.psum_scatter(
            qkv_total.astype(jnp.bfloat16), "dp", scatter_dimension=0, tiled=True
        ).astype(jnp.float32),
        lax.psum_scatter(
            out_total.astype(jnp.bfloat16), "dp", scatter_dimension=1, tiled=True
        ).astype(jnp.float32),
        lax.psum_scatter(
            up_total.astype(jnp.bfloat16), "dp", scatter_dimension=0, tiled=True
        ).astype(jnp.float32),
        lax.psum_scatter(
            down_total.astype(jnp.bfloat16), "dp", scatter_dimension=1, tiled=True
        ).astype(jnp.float32),
    )
    return (
        layer_outputs,
        input_grads,
        gains_grad[None],
        qkv_grad[None],
        out_grad[None],
        up_grad[None],
        down_grad[None],
    )


def solution(mesh):
    placed = (
        P("dp", "tensor", None),
        P("dp", "tensor", None),
        P("dp", "tensor"),
        P(),
        P("section", None, None),
        P("section", None, None, "tensor"),
        P("section", "tensor", None),
        P("section", None, "tensor"),
        P("section", "tensor", None),
    )
    return jax.shard_map(
        per_device,
        mesh=mesh,
        in_specs=placed,
        out_specs=(
            P("section", "dp", "tensor", None),
            P("section", "dp", "tensor", None),
            P("section", None, ("dp", "tensor")),
            P("section", "dp", None, "tensor"),
            P("section", "tensor", "dp"),
            P("section", "dp", "tensor"),
            P("section", "tensor", "dp"),
        ),
        check_vma=False,
    )
```

profile of v0, /device:TPU:0, one launch (start us, length us, event | category | flops | bytes accessed | tf_op | source)
XLA Modules:
  0.0 2998.0 jit_solution(8786126189976020737)
XLA Ops:
  16.6 925.6 %while.41 = (s32[]{:T(128)}, bf16[256,1024]{1,0:T(8,128)(2,1)S(1)}, bf16[3,256,1024]{2,1,0:T(8,128)(2,1)}, bf16[3,256,1024]{2,1,0:T(8,128)(2,1)}, pred[]{:T(512)...) while((s32[]{:T(128)}, bf16[256,1024]{1,0:T(8,128)(2,1)S(1)}, ...), condition=%wide.region_9.10_spmd, body=%wide.region_0.9_spmd.sunk | while | flops 7564986880 | bytes 155824272 | solution.py:247
  20.9 47.9 %all-gather.7.cloned.1.call-done = bf16[1024,1024]{1,0:T(8,128)(2,1)} async-done(((bf16[256,1024]{1,0:T(8,128)(2,1)}), bf16[1024,1024]{1,0:T(8,128)(2,1)}) %all-gather.7.cloned.1.call-update) | async-done | bytes 2097168 | tf_op jit(solution)/shard_map/while/body/eval_jaxpr/all_gather | solution.py:55
  95.7 75.6 %reduce-scatter.24.cloned.1.call-done = f32[256,1024]{1,0:T(8,128)} async-done(((f32[1024,1024]{1,0:T(8,128)}), f32[256,1024]{1,0:T(8,128)}) %reduce-scatter.24.cloned.1.call-update) | async-done | bytes 1048592 | tf_op jit(solution)/shard_map/while/body/eval_jaxpr/reduce_scatter | solution.py:63
  231.9 75.6 %reduce-scatter.26.cloned.1.call-done = f32[256,1024]{1,0:T(8,128)} async-done(((f32[1024,1024]{1,0:T(8,128)}), f32[256,1024]{1,0:T(8,128)}) %reduce-scatter.26.cloned.1.call-update) | async-done | bytes 1048592 | tf_op jit(solution)/shard_map/while/body/eval_jaxpr/reduce_scatter | solution.py:63
  330.2 46.7 %all-gather.7.cloned.1.call-done = bf16[1024,1024]{1,0:T(8,128)(2,1)} async-done(((bf16[256,1024]{1,0:T(8,128)(2,1)}), bf16[1024,1024]{1,0:T(8,128)(2,1)}) %all-gather.7.cloned.1.call-update) | async-done | bytes 2097168 | tf_op jit(solution)/shard_map/while/body/eval_jaxpr/all_gather | solution.py:55
  403.8 75.6 %reduce-scatter.24.cloned.1.call-done = f32[256,1024]{1,0:T(8,128)} async-done(((f32[1024,1024]{1,0:T(8,128)}), f32[256,1024]{1,0:T(8,128)}) %reduce-scatter.24.cloned.1.call-update) | async-done | bytes 1048592 | tf_op jit(solution)/shard_map/while/body/eval_jaxpr/reduce_scatter | solution.py:63
  540.1 75.6 %reduce-scatter.26.cloned.1.call-done = f32[256,1024]{1,0:T(8,128)} async-done(((f32[1024,1024]{1,0:T(8,128)}), f32[256,1024]{1,0:T(8,128)}) %reduce-scatter.26.cloned.1.call-update) | async-done | bytes 1048592 | tf_op jit(solution)/shard_map/while/body/eval_jaxpr/reduce_scatter | solution.py:63
  638.4 46.7 %all-gather.7.cloned.1.call-done = bf16[1024,1024]{1,0:T(8,128)(2,1)} async-done(((bf16[256,1024]{1,0:T(8,128)(2,1)}), bf16[1024,1024]{1,0:T(8,128)(2,1)}) %all-gather.7.cloned.1.call-update) | async-done | bytes 2097168 | tf_op jit(solution)/shard_map/while/body/eval_jaxpr/all_gather | solution.py:55
  712.0 75.6 %reduce-scatter.24.cloned.1.call-done = f32[256,1024]{1,0:T(8,128)} async-done(((f32[1024,1024]{1,0:T(8,128)}), f32[256,1024]{1,0:T(8,128)}) %reduce-scatter.24.cloned.1.call-update) | async-done | bytes 1048592 | tf_op jit(solution)/shard_map/while/body/eval_jaxpr/reduce_scatter | solution.py:63
  848.3 75.6 %reduce-scatter.26.cloned.1.call-done = f32[256,1024]{1,0:T(8,128)} async-done(((f32[1024,1024]{1,0:T(8,128)}), f32[256,1024]{1,0:T(8,128)}) %reduce-scatter.26.cloned.1.call-update) | async-done | bytes 1048592 | tf_op jit(solution)/shard_map/while/body/eval_jaxpr/reduce_scatter | solution.py:63
  948.0 1857.8 %while.42 = (s32[]{:T(128)}, bf16[256,1024]{1,0:T(8,128)(2,1)S(1)}, f32[4,1024]{1,0:T(4,128)S(1)}, f32[1024,3,256]{2,0,1:T(8,128)}, f32[256,1024]{1,0:T(8,128)},...) while((s32[]{:T(128)}, bf16[256,1024]{1,0:T(8,128)(2,1)S(1)}, ...), condition=%wide.region_31.32_spmd.clone, body=%wide.region_11.31_spmd.clone.sunk | while | flops 22695434240 | bytes 623419904 | solution.py:276
  950.4 48.2 %all-gather.11.cloned.1.call-done = bf16[1024,1024]{1,0:T(8,128)(2,1)} async-done(((bf16[256,1024]{1,0:T(8,128)(2,1)}), bf16[1024,1024]{1,0:T(8,128)(2,1)}) %all-gather.11.cloned.1.call-update) | async-done | bytes 2097168 | tf_op jit(solution)/shard_map/while/body/eval_jaxpr/all_gather | solution.py:55
  1027.8 75.6 %reduce-scatter.28.cloned.1.call-done = f32[256,1024]{1,0:T(8,128)} async-done(((f32[1024,1024]{1,0:T(8,128)}), f32[256,1024]{1,0:T(8,128)}) %reduce-scatter.28.cloned.1.call-update) | async-done | bytes 1048592 | tf_op jit(solution)/shard_map/while/body/eval_jaxpr/reduce_scatter | solution.py:63
  1165.3 75.6 %reduce-scatter.30.cloned.1.call-done = f32[256,1024]{1,0:T(8,128)} async-done(((f32[1024,1024]{1,0:T(8,128)}), f32[256,1024]{1,0:T(8,128)}) %reduce-scatter.30.cloned.1.call-update) | async-done | bytes 1048592 | tf_op jit(solution)/shard_map/while/body/eval_jaxpr/reduce_scatter | solution.py:63
  1306.9 75.6 %reduce-scatter.32.cloned.1.call-done = f32[256,1024]{1,0:T(8,128)} async-done(((f32[1024,1024]{1,0:T(8,128)}), f32[256,1024]{1,0:T(8,128)}) %reduce-scatter.32.cloned.1.call-update) | async-done | bytes 1048592 | tf_op jit(solution)/shard_map/while/body/eval_jaxpr/reduce_scatter | solution.py:84
  1491.5 56.0 %reduce-scatter.34.cloned.1.call-done = f32[256,1024]{1,0:T(8,128)} async-done(((f32[1024,1024]{1,0:T(8,128)}), f32[256,1024]{1,0:T(8,128)}) %reduce-scatter.34.cloned.1.call-update) | async-done | bytes 1048592 | tf_op jit(solution)/shard_map/while/body/eval_jaxpr/reduce_scatter | solution.py:84
  1645.8 75.6 %reduce-scatter.28.cloned.1.call-done = f32[256,1024]{1,0:T(8,128)} async-done(((f32[1024,1024]{1,0:T(8,128)}), f32[256,1024]{1,0:T(8,128)}) %reduce-scatter.28.cloned.1.call-update) | async-done | bytes 1048592 | tf_op jit(solution)/shard_map/while/body/eval_jaxpr/reduce_scatter | solution.py:63
  1783.3 75.6 %reduce-scatter.30.cloned.1.call-done = f32[256,1024]{1,0:T(8,128)} async-done(((f32[1024,1024]{1,0:T(8,128)}), f32[256,1024]{1,0:T(8,128)}) %reduce-scatter.30.cloned.1.call-update) | async-done | bytes 1048592 | tf_op jit(solution)/shard_map/while/body/eval_jaxpr/reduce_scatter | solution.py:63
  1924.9 75.6 %reduce-scatter.32.cloned.1.call-done = f32[256,1024]{1,0:T(8,128)} async-done(((f32[1024,1024]{1,0:T(8,128)}), f32[256,1024]{1,0:T(8,128)}) %reduce-scatter.32.cloned.1.call-update) | async-done | bytes 1048592 | tf_op jit(solution)/shard_map/while/body/eval_jaxpr/reduce_scatter | solution.py:84
  2113.3 52.2 %reduce-scatter.34.cloned.1.call-done = f32[256,1024]{1,0:T(8,128)} async-done(((f32[1024,1024]{1,0:T(8,128)}), f32[256,1024]{1,0:T(8,128)}) %reduce-scatter.34.cloned.1.call-update) | async-done | bytes 1048592 | tf_op jit(solution)/shard_map/while/body/eval_jaxpr/reduce_scatter | solution.py:84
  2263.8 75.6 %reduce-scatter.28.cloned.1.call-done = f32[256,1024]{1,0:T(8,128)} async-done(((f32[1024,1024]{1,0:T(8,128)}), f32[256,1024]{1,0:T(8,128)}) %reduce-scatter.28.cloned.1.call-update) | async-done | bytes 1048592 | tf_op jit(solution)/shard_map/while/body/eval_jaxpr/reduce_scatter | solution.py:63
  2401.3 75.6 %reduce-scatter.30.cloned.1.call-done = f32[256,1024]{1,0:T(8,128)} async-done(((f32[1024,1024]{1,0:T(8,128)}), f32[256,1024]{1,0:T(8,128)}) %reduce-scatter.30.cloned.1.call-update) | async-done | bytes 1048592 | tf_op jit(solution)/shard_map/while/body/eval_jaxpr/reduce_scatter | solution.py:63
  2542.8 75.6 %reduce-scatter.32.cloned.1.call-done = f32[256,1024]{1,0:T(8,128)} async-done(((f32[1024,1024]{1,0:T(8,128)}), f32[256,1024]{1,0:T(8,128)}) %reduce-scatter.32.cloned.1.call-update) | async-done | bytes 1048592 | tf_op jit(solution)/shard_map/while/body/eval_jaxpr/reduce_scatter | solution.py:84
  2731.0 52.4 %reduce-scatter.34.cloned.1.call-done = f32[256,1024]{1,0:T(8,128)} async-done(((f32[1024,1024]{1,0:T(8,128)}), f32[256,1024]{1,0:T(8,128)}) %reduce-scatter.34.cloned.1.call-update) | async-done | bytes 1048592 | tf_op jit(solution)/shard_map/while/body/eval_jaxpr/reduce_scatter | solution.py:84
  (575 shorter events, 1493.3 us)
Async XLA Ops:
  19.9 151.3 %reduce-scatter.24.cloned.1.call-start = ((), (), s32[]{:S(2)}) async-start(), calls=%async_computation.17 | async-start | bytes 5242880 | tf_op jit(solution)/shard_map/while/body/eval_jaxpr/reduce_scatter | solution.py:63
  176.6 131.0 %reduce-scatter.26.cloned.1.call-start = ((), (), s32[]{:S(2)}) async-start(), calls=%async_computation.19 | async-start | bytes 5242880 | tf_op jit(solution)/shard_map/while/body/eval_jaxpr/reduce_scatter | solution.py:63
  329.2 150.2 %reduce-scatter.24.cloned.1.call-start = ((), (), s32[]{:S(2)}) async-start(), calls=%async_computation.17 | async-start | bytes 5242880 | tf_op jit(solution)/shard_map/while/body/eval_jaxpr/reduce_scatter | solution.py:63
  484.7 131.0 %reduce-scatter.26.cloned.1.call-start = ((), (), s32[]{:S(2)}) async-start(), calls=%async_computation.19 | async-start | bytes 5242880 | tf_op jit(solution)/shard_map/while/body/eval_jaxpr/reduce_scatter | solution.py:63
  637.5 150.2 %reduce-scatter.24.cloned.1.call-start = ((), (), s32[]{:S(2)}) async-start(), calls=%async_computation.17 | async-start | bytes 5242880 | tf_op jit(solution)/shard_map/while/body/eval_jaxpr/reduce_scatter | solution.py:63
  712.0 127.6 %all-gather.9.cloned.1.call-start = ((), (), s32[]{:S(2)}) async-start(), calls=%async_computation.18 | async-start | bytes 2621440 | tf_op jit(solution)/shard_map/while/body/eval_jaxpr/all_gather | solution.py:55
  793.0 131.0 %reduce-scatter.26.cloned.1.call-start = ((), (), s32[]{:S(2)}) async-start(), calls=%async_computation.19 | async-start | bytes 5242880 | tf_op jit(solution)/shard_map/while/body/eval_jaxpr/reduce_scatter | solution.py:63
  949.5 153.9 %reduce-scatter.28.cloned.1.call-start = ((), (), s32[]{:S(2)}) async-start(), calls=%async_computation.21 | async-start | bytes 5242880 | tf_op jit(solution)/shard_map/while/body/eval_jaxpr/reduce_scatter | solution.py:63
  1107.4 133.5 %reduce-scatter.30.cloned.1.call-start = ((), (), s32[]{:S(2)}) async-start(), calls=%async_computation.23 | async-start | bytes 5242880 | tf_op jit(solution)/shard_map/while/body/eval_jaxpr/reduce_scatter | solution.py:63
  1165.2 128.0 %all-gather.15.cloned.1.call-start = ((), (), s32[]{:S(2)}) async-start(), calls=%async_computation.24 | async-start | bytes 2621440 | tf_op jit(solution)/shard_map/while/body/eval_jaxpr/all_gather | solution.py:76
  1246.6 135.8 %reduce-scatter.32.cloned.1.call-start = ((), (), s32[]{:S(2)}) async-start(), calls=%async_computation.25 | async-start | bytes 5242880 | tf_op jit(solution)/shard_map/while/body/eval_jaxpr/reduce_scatter | solution.py:84
  1387.3 160.2 %reduce-scatter.34.cloned.1.call-start = ((), (), s32[]{:S(2)}) async-start(), calls=%async_computation.27 | async-start | bytes 5242880 | tf_op jit(solution)/shard_map/while/body/eval_jaxpr/reduce_scatter | solution.py:84
  1569.4 152.0 %reduce-scatter.28.cloned.1.call-start = ((), (), s32[]{:S(2)}) async-start(), calls=%async_computation.21 | async-start | bytes 5242880 | tf_op jit(solution)/shard_map/while/body/eval_jaxpr/reduce_scatter | solution.py:63
  1725.4 133.5 %reduce-scatter.30.cloned.1.call-start = ((), (), s32[]{:S(2)}) async-start(), calls=%async_computation.23 | async-start | bytes 5242880 | tf_op jit(solution)/shard_map/while/body/eval_jaxpr/reduce_scatter | solution.py:63
  1783.3 128.0 %all-gather.15.cloned.1.call-start = ((), (), s32[]{:S(2)}) async-start(), calls=%async_computation.24 | async-start | bytes 2621440 | tf_op jit(solution)/shard_map/while/body/eval_jaxpr/all_gather | solution.py:76
  1864.6 135.8 %reduce-scatter.32.cloned.1.call-start = ((), (), s32[]{:S(2)}) async-start(), calls=%async_computation.25 | async-start | bytes 5242880 | tf_op jit(solution)/shard_map/while/body/eval_jaxpr/reduce_scatter | solution.py:84
  2005.4 160.2 %reduce-scatter.34.cloned.1.call-start = ((), (), s32[]{:S(2)}) async-start(), calls=%async_computation.27 | async-start | bytes 5242880 | tf_op jit(solution)/shard_map/while/body/eval_jaxpr/reduce_scatter | solution.py:84
  2187.3 152.0 %reduce-scatter.28.cloned.1.call-start = ((), (), s32[]{:S(2)}) async-start(), calls=%async_computation.21 | async-start | bytes 5242880 | tf_op jit(solution)/shard_map/while/body/eval_jaxpr/reduce_scatter | solution.py:63
  2343.3 133.5 %reduce-scatter.30.cloned.1.call-start = ((), (), s32[]{:S(2)}) async-start(), calls=%async_computation.23 | async-start | bytes 5242880 | tf_op jit(solution)/shard_map/while/body/eval_jaxpr/reduce_scatter | solution.py:63
  2401.2 128.0 %all-gather.15.cloned.1.call-start = ((), (), s32[]{:S(2)}) async-start(), calls=%async_computation.24 | async-start | bytes 2621440 | tf_op jit(solution)/shard_map/while/body/eval_jaxpr/all_gather | solution.py:76
  2482.6 135.8 %reduce-scatter.32.cloned.1.call-start = ((), (), s32[]{:S(2)}) async-start(), calls=%async_computation.25 | async-start | bytes 5242880 | tf_op jit(solution)/shard_map/while/body/eval_jaxpr/reduce_scatter | solution.py:84
  2623.3 160.2 %reduce-scatter.34.cloned.1.call-start = ((), (), s32[]{:S(2)}) async-start(), calls=%async_computation.27 | async-start | bytes 5242880 | tf_op jit(solution)/shard_map/while/body/eval_jaxpr/reduce_scatter | solution.py:84
  2812.4 141.8 %reduce-scatter.20.cloned.1.call-start = ((), (), s32[]{:S(2)}) async-start(), calls=%async_computation.14 | async-start | bytes 2621440 | tf_op jit(solution)/shard_map/reduce_scatter | solution.py:294
  2816.3 171.8 %reduce-scatter.18.cloned.1.call-start = ((), (), s32[]{:S(2)}) async-start(), calls=%async_computation.13 | async-start | bytes 2621440 | tf_op jit(solution)/shard_map/reduce_scatter | solution.py:291
  (127 other events, 4695.7 us)
Sparse Core Ops, SparseCore 0:
  20.0 48.6 all-gather.6
  95.7 75.4 reduce-scatter.23
  232.1 75.4 reduce-scatter.25
  329.4 47.4 all-gather.6
  403.9 75.4 reduce-scatter.23
  540.2 75.4 reduce-scatter.25
  637.6 47.4 all-gather.6
  712.1 75.4 reduce-scatter.23
  848.4 75.4 reduce-scatter.25
  951.1 47.4 all-gather.10
  1027.9 75.4 reduce-scatter.27
  1165.4 75.4 reduce-scatter.29
  1306.9 75.4 reduce-scatter.31
  1387.4 46.4 all-gather.16
  1472.0 75.4 reduce-scatter.33
  1645.9 75.4 reduce-scatter.27
  1783.4 75.4 reduce-scatter.29
  1925.0 75.4 reduce-scatter.31
  2005.5 46.4 all-gather.16
  2090.0 75.4 reduce-scatter.33
  2263.8 75.4 reduce-scatter.27
  2401.3 75.4 reduce-scatter.29
  2542.9 75.4 reduce-scatter.31
  2707.9 75.4 reduce-scatter.33
  (12 shorter events, 555.0 us)
Sparse Core Ops, SparseCore 1:
  2810.4 55.4 reduce-scatter.21
  2868.9 20.5 reduce-scatter.15
  2892.0 28.1 reduce-scatter.13
  2922.8 31.3 reduce-scatter.19
  2956.7 31.3 reduce-scatter.17
where the time goes:
time: 3010 us; the launch traced here: 3000 us
  waiting for transfers between devices  2350 us (78%)
  matrix products  391 us (13%)
  other arithmetic  161 us (5%)
  local copies, waits for them, and re-layouts  45.5 us (2%)
    reduce_scatter x12, waiting for transfers between devices, scatter_rows(): lax.psum_scatter(partial_term(jnp.int32(0), lax.axis_size('tensor') * row...  907 us
    all_gather x12, waiting for transfers between devices, gather_rows(): lax.all_gather(row_values, 'tensor', axis=0, tiled=True)  549 us
    reduce_scatter x6, waiting for transfers between devices, scatter_grads(): lax.psum_scatter(partial_term(jnp.int32(0), lax.axis_size('tensor') * row...  387 us
    all_gather x6, waiting for transfers between devices, gather_grads(): lax.all_gather(row_values, 'tensor', axis=0, tiled=True)  279 us
    ppermute x6, waiting for transfers between devices, shifted(): return lax.ppermute(block, axis, route)  69.5 us
    dot_general x12, matrix products, contract(): lax.dot_general(left_rows, right_rows, (((0,), (0,)), ((), ())), preferre...  63 us
    sub x6, matrix products, attention_probs(): expos = jnp.exp(scores - jnp.max(scores, axis=-1, keepdims=True))  62.7 us
    dot_general x12, matrix products, partial_term(): return jnp.dot(row_values, weight, preferred_element_type=jnp.float32)  62.4 us
  transfers between devices with their start and end apart: 47, of which 47 were waited for; matrix products, arithmetic and copies ran while one was open for 3% of the time, Pallas kernels for 0%

commit v1 on v0

--- a/solution.py
+++ b/solution.py
@@ -49,10 +49,40 @@
 
 def gather_rows(row_values, weight):
 
+    def _pass_threads(local_values, mesh_dim="tensor"):
+        f_now, state_next, arr_next = (
+            lax.psum(1, mesh_dim),
+            lax.axis_index(mesh_dim),
+            local_values.shape[0],
+        )
+        slots = []
+        for src_i in range(f_now):
+            slots.append((src_i, (src_i + 1) % f_now))
+        leaves = []
+        for src_i in range(f_now):
+            leaves.append((src_i, (src_i - 1) % f_now))
+        w1 = jnp.zeros(
+            (*local_values.shape[:0], f_now * arr_next, *local_values.shape[1:]), local_values.dtype
+        )
+        w1 = lax.dynamic_update_slice_in_dim(w1, local_values, state_next * arr_next, axis=0)
+        vec_out = f_now // 2
+        block_next = top = local_values
+        for dd in range(1, vec_out + 1):
+            block_next = lax.ppermute(block_next, mesh_dim, slots)
+            w1 = lax.dynamic_update_slice_in_dim(
+                w1, block_next, (state_next - dd) % f_now * arr_next, axis=0
+            )
+            if dd < f_now - vec_out:
+                top = lax.ppermute(top, mesh_dim, leaves)
+                w1 = lax.dynamic_update_slice_in_dim(
+                    w1, top, (state_next + dd) % f_now * arr_next, axis=0
+                )
+        return w1
+
     def project(shard_rows, offset):
         return (shard_rows, jnp.dot(shard_rows, weight, preferred_element_type=jnp.float32))
 
-    return project(lax.all_gather(row_values, "tensor", axis=0, tiled=True), jnp.int32(0))
+    return project(_pass_threads(row_values), jnp.int32(0))
 
 
 def scatter_rows(row_values, weight, row_count):

time: 3010 us -> 2920 us (0.970)
  waiting for transfers between devices: 2350 us -> 2060 us
  starting transfers between devices: 28.6 us -> 153 us
  local copies, waits for them, and re-layouts: 45.5 us -> 124 us
    all_gather x12 -> x0, waiting for transfers between devices: 549 us -> none  [gather_rows(): lax.all_gather(row_values, 'tensor', axis=0, tiled=True)]
    ppermute x0 -> x36, waiting for transfers between devices: none -> 256 us  [the longest x24 237 us: _pass_threads(): block_next = lax.ppermute(block_next, mesh_dim, slots)]
    ppermute x0 -> x36, starting transfers between devices: none -> 138 us  [the longest x24 110 us: _pass_threads(): block_next = lax.ppermute(block_next, mesh_dim, slots)]
    dynamic_update_slice x0 -> x42, local copies, waits for them, and re-layouts: none -> 38 us  [the longest x24 21.9 us: _pass_threads(): lax.dynamic_update_slice_in_dim(w1, block_next, (state_next - dd) % f_now...]
  transfers between devices with their start and end apart: 47 -> 71, of which waited for: 47 -> 68; matrix products, arithmetic and copies ran while one was open for 3% -> 5% of each run, Pallas kernels for 0% -> 0%
where the time goes in v1:
time: 2920 us; the launch traced here: 2900 us
  waiting for transfers between devices  2060 us (71%)
  matrix products  389 us (13%)
  other arithmetic  154 us (5%)
  starting transfers between devices  153 us (5%)
  local copies, waits for them, and re-layouts  124 us (4%)
    reduce_scatter x12, waiting for transfers between devices, scatter_rows(): lax.psum_scatter(partial_term(jnp.int32(0), lax.axis_size('tensor') * row...  911 us
    reduce_scatter x6, waiting for transfers between devices, scatter_grads(): lax.psum_scatter(partial_term(jnp.int32(0), lax.axis_size('tensor') * row...  386 us
    all_gather x6, waiting for transfers between devices, gather_grads(): lax.all_gather(row_values, 'tensor', axis=0, tiled=True)  279 us
    ppermute x24, waiting for transfers between devices, _pass_threads(): block_next = lax.ppermute(block_next, mesh_dim, slots)  237 us
    ppermute x24, starting transfers between devices, _pass_threads(): block_next = lax.ppermute(block_next, mesh_dim, slots)  110 us
    ppermute x6, waiting for transfers between devices, shifted(): return lax.ppermute(block, axis, route)  69.4 us
    dot_general x12, matrix products, partial_term(): return jnp.dot(row_values, weight, preferred_element_type=jnp.float32)  64.6 us
    dot_general x12, matrix products, contract(): lax.dot_general(left_rows, right_rows, (((0,), (0,)), ((), ())), preferre...  64.2 us
  transfers between devices with their start and end apart: 71, of which 68 were waited for; matrix products, arithmetic and copies ran while one was open for 5% of the time, Pallas kernels for 0%

profile of v1, /device:TPU:0, one launch (start us, length us, event | category | flops | bytes accessed | tf_op | source)
XLA Modules:
  0.0 2903.3 jit_solution(3991799308101972285)
XLA Ops:
  15.4 876.5 %while.41 = (s32[]{:T(128)}, bf16[256,1024]{1,0:T(8,128)(2,1)S(1)}, bf16[3,256,1024]{2,1,0:T(8,128)(2,1)}, bf16[3,256,1024]{2,1,0:T(8,128)(2,1)}, pred[]{:T(512)...) while((s32[]{:T(128)}, bf16[256,1024]{1,0:T(8,128)(2,1)S(1)}, ...), condition=%wide.region_9.10_spmd, body=%wide.region_0.9_spmd.sunk | while | flops 7564986880 | bytes 166310864 | solution.py:277
  84.2 76.2 %reduce-scatter.24.cloned.1.call-done = f32[256,1024]{1,0:T(8,128)} async-done(((f32[1024,1024]{1,0:T(8,128)}), f32[256,1024]{1,0:T(8,128)}) %reduce-scatter.24.cloned.1.call-update) | async-done | bytes 1048592 | tf_op jit(solution)/shard_map/while/body/eval_jaxpr/reduce_scatter | solution.py:93
  214.5 76.0 %reduce-scatter.26.cloned.1.call-done = f32[256,1024]{1,0:T(8,128)} async-done(((f32[1024,1024]{1,0:T(8,128)}), f32[256,1024]{1,0:T(8,128)}) %reduce-scatter.26.cloned.1.call-update) | async-done | bytes 1048592 | tf_op jit(solution)/shard_map/while/body/eval_jaxpr/reduce_scatter | solution.py:93
  375.3 76.6 %reduce-scatter.24.cloned.1.call-done = f32[256,1024]{1,0:T(8,128)} async-done(((f32[1024,1024]{1,0:T(8,128)}), f32[256,1024]{1,0:T(8,128)}) %reduce-scatter.24.cloned.1.call-update) | async-done | bytes 1048592 | tf_op jit(solution)/shard_map/while/body/eval_jaxpr/reduce_scatter | solution.py:93
  506.0 76.0 %reduce-scatter.26.cloned.1.call-done = f32[256,1024]{1,0:T(8,128)} async-done(((f32[1024,1024]{1,0:T(8,128)}), f32[256,1024]{1,0:T(8,128)}) %reduce-scatter.26.cloned.1.call-update) | async-done | bytes 1048592 | tf_op jit(solution)/shard_map/while/body/eval_jaxpr/reduce_scatter | solution.py:93
  666.8 76.6 %reduce-scatter.24.cloned.1.call-done = f32[256,1024]{1,0:T(8,128)} async-done(((f32[1024,1024]{1,0:T(8,128)}), f32[256,1024]{1,0:T(8,128)}) %reduce-scatter.24.cloned.1.call-update) | async-done | bytes 1048592 | tf_op jit(solution)/shard_map/while/body/eval_jaxpr/reduce_scatter | solution.py:93
  797.5 76.0 %reduce-scatter.26.cloned.1.call-done = f32[256,1024]{1,0:T(8,128)} async-done(((f32[1024,1024]{1,0:T(8,128)}), f32[256,1024]{1,0:T(8,128)}) %reduce-scatter.26.cloned.1.call-update) | async-done | bytes 1048592 | tf_op jit(solution)/shard_map/while/body/eval_jaxpr/reduce_scatter | solution.py:93
  897.6 1813.5 %while.42 = (s32[]{:T(128)}, bf16[256,1024]{1,0:T(8,128)(2,1)S(1)}, f32[4,1024]{1,0:T(4,128)}, f32[1024,3,256]{2,0,1:T(8,128)}, f32[256,1024]{1,0:T(8,128)}, /*i...) while((s32[]{:T(128)}, bf16[256,1024]{1,0:T(8,128)(2,1)S(1)}, ...), condition=%wide.region_31.32_spmd.clone, body=%wide.region_11.31_spmd.clone.sunk | while | flops 22695434240 | bytes 637363712 | solution.py:306
  967.5 76.5 %reduce-scatter.28.cloned.1.call-done = f32[256,1024]{1,0:T(8,128)} async-done(((f32[1024,1024]{1,0:T(8,128)}), f32[256,1024]{1,0:T(8,128)}) %reduce-scatter.28.cloned.1.call-update) | async-done | bytes 1048592 | tf_op jit(solution)/shard_map/while/body/eval_jaxpr/reduce_scatter | solution.py:93
  1099.1 76.0 %reduce-scatter.30.cloned.1.call-done = f32[256,1024]{1,0:T(8,128)} async-done(((f32[1024,1024]{1,0:T(8,128)}), f32[256,1024]{1,0:T(8,128)}) %reduce-scatter.30.cloned.1.call-update) | async-done | bytes 1048592 | tf_op jit(solution)/shard_map/while/body/eval_jaxpr/reduce_scatter | solution.py:93
  1180.8 46.6 %all-gather.3.cloned.1.call-done = bf16[1024,1024]{1,0:T(8,128)(2,1)} async-done(((bf16[256,1024]{1,0:T(8,128)(2,1)}), bf16[1024,1024]{1,0:T(8,128)(2,1)}) %all-gather.3.cloned.1.call-update) | async-done | bytes 2097168 | tf_op jit(solution)/shard_map/while/body/eval_jaxpr/all_gather | solution.py:106
  1241.1 75.6 %reduce-scatter.32.cloned.1.call-done = f32[256,1024]{1,0:T(8,128)} async-done(((f32[1024,1024]{1,0:T(8,128)}), f32[256,1024]{1,0:T(8,128)}) %reduce-scatter.32.cloned.1.call-update) | async-done | bytes 1048592 | tf_op jit(solution)/shard_map/while/body/eval_jaxpr/reduce_scatter | solution.py:114
  1321.6 46.5 %all-gather.5.cloned.1.call-done = bf16[1024,1024]{1,0:T(8,128)(2,1)} async-done(((bf16[256,1024]{1,0:T(8,128)(2,1)}), bf16[1024,1024]{1,0:T(8,128)(2,1)}) %all-gather.5.cloned.1.call-update) | async-done | bytes 2097168 | tf_op jit(solution)/shard_map/while/body/eval_jaxpr/all_gather | solution.py:106
  1427.3 54.8 %reduce-scatter.34.cloned.1.call-done = f32[256,1024]{1,0:T(8,128)} async-done(((f32[1024,1024]{1,0:T(8,128)}), f32[256,1024]{1,0:T(8,128)}) %reduce-scatter.34.cloned.1.call-update) | async-done | bytes 1048592 | tf_op jit(solution)/shard_map/while/body/eval_jaxpr/reduce_scatter | solution.py:114
  1572.6 74.7 %reduce-scatter.28.cloned.1.call-done = f32[256,1024]{1,0:T(8,128)} async-done(((f32[1024,1024]{1,0:T(8,128)}), f32[256,1024]{1,0:T(8,128)}) %reduce-scatter.28.cloned.1.call-update) | async-done | bytes 1048592 | tf_op jit(solution)/shard_map/while/body/eval_jaxpr/reduce_scatter | solution.py:93
  1702.3 76.0 %reduce-scatter.30.cloned.1.call-done = f32[256,1024]{1,0:T(8,128)} async-done(((f32[1024,1024]{1,0:T(8,128)}), f32[256,1024]{1,0:T(8,128)}) %reduce-scatter.30.cloned.1.call-update) | async-done | bytes 1048592 | tf_op jit(solution)/shard_map/while/body/eval_jaxpr/reduce_scatter | solution.py:93
  1844.3 75.6 %reduce-scatter.32.cloned.1.call-done = f32[256,1024]{1,0:T(8,128)} async-done(((f32[1024,1024]{1,0:T(8,128)}), f32[256,1024]{1,0:T(8,128)}) %reduce-scatter.32.cloned.1.call-update) | async-done | bytes 1048592 | tf_op jit(solution)/shard_map/while/body/eval_jaxpr/reduce_scatter | solution.py:114
  1924.8 46.6 %all-gather.5.cloned.1.call-done = bf16[1024,1024]{1,0:T(8,128)(2,1)} async-done(((bf16[256,1024]{1,0:T(8,128)(2,1)}), bf16[1024,1024]{1,0:T(8,128)(2,1)}) %all-gather.5.cloned.1.call-update) | async-done | bytes 2097168 | tf_op jit(solution)/shard_map/while/body/eval_jaxpr/all_gather | solution.py:106
  2033.4 52.2 %reduce-scatter.34.cloned.1.call-done = f32[256,1024]{1,0:T(8,128)} async-done(((f32[1024,1024]{1,0:T(8,128)}), f32[256,1024]{1,0:T(8,128)}) %reduce-scatter.34.cloned.1.call-update) | async-done | bytes 1048592 | tf_op jit(solution)/shard_map/while/body/eval_jaxpr/reduce_scatter | solution.py:114
  2175.9 74.7 %reduce-scatter.28.cloned.1.call-done = f32[256,1024]{1,0:T(8,128)} async-done(((f32[1024,1024]{1,0:T(8,128)}), f32[256,1024]{1,0:T(8,128)}) %reduce-scatter.28.cloned.1.call-update) | async-done | bytes 1048592 | tf_op jit(solution)/shard_map/while/body/eval_jaxpr/reduce_scatter | solution.py:93
  2305.5 76.0 %reduce-scatter.30.cloned.1.call-done = f32[256,1024]{1,0:T(8,128)} async-done(((f32[1024,1024]{1,0:T(8,128)}), f32[256,1024]{1,0:T(8,128)}) %reduce-scatter.30.cloned.1.call-update) | async-done | bytes 1048592 | tf_op jit(solution)/shard_map/while/body/eval_jaxpr/reduce_scatter | solution.py:93
  2447.6 75.6 %reduce-scatter.32.cloned.1.call-done = f32[256,1024]{1,0:T(8,128)} async-done(((f32[1024,1024]{1,0:T(8,128)}), f32[256,1024]{1,0:T(8,128)}) %reduce-scatter.32.cloned.1.call-update) | async-done | bytes 1048592 | tf_op jit(solution)/shard_map/while/body/eval_jaxpr/reduce_scatter | solution.py:114
  2528.1 46.6 %all-gather.5.cloned.1.call-done = bf16[1024,1024]{1,0:T(8,128)(2,1)} async-done(((bf16[256,1024]{1,0:T(8,128)(2,1)}), bf16[1024,1024]{1,0:T(8,128)(2,1)}) %all-gather.5.cloned.1.call-update) | async-done | bytes 2097168 | tf_op jit(solution)/shard_map/while/body/eval_jaxpr/all_gather | solution.py:106
  2636.4 52.2 %reduce-scatter.34.cloned.1.call-done = f32[256,1024]{1,0:T(8,128)} async-done(((f32[1024,1024]{1,0:T(8,128)}), f32[256,1024]{1,0:T(8,128)}) %reduce-scatter.34.cloned.1.call-update) | async-done | bytes 1048592 | tf_op jit(solution)/shard_map/while/body/eval_jaxpr/reduce_scatter | solution.py:114
  (755 shorter events, 1398.3 us)
Async XLA Ops:
  15.4 145.0 %reduce-scatter.24.cloned.1.call-start = ((), (), s32[]{:S(2)}) async-start(), calls=%async_computation.16 | async-start | bytes 5242880 | tf_op jit(solution)/shard_map/while/body/eval_jaxpr/reduce_scatter | solution.py:93
  84.1 206.4 %reduce-scatter.26.cloned.1.call-start = ((), (), s32[]{:S(2)}) async-start(), calls=%async_computation.17 | async-start | bytes 5242880 | tf_op jit(solution)/shard_map/while/body/eval_jaxpr/reduce_scatter | solution.py:93
  308.8 143.0 %reduce-scatter.24.cloned.1.call-start = ((), (), s32[]{:S(2)}) async-start(), calls=%async_computation.16 | async-start | bytes 5242880 | tf_op jit(solution)/shard_map/while/body/eval_jaxpr/reduce_scatter | solution.py:93
  375.2 206.8 %reduce-scatter.26.cloned.1.call-start = ((), (), s32[]{:S(2)}) async-start(), calls=%async_computation.17 | async-start | bytes 5242880 | tf_op jit(solution)/shard_map/while/body/eval_jaxpr/reduce_scatter | solution.py:93
  600.3 143.1 %reduce-scatter.24.cloned.1.call-start = ((), (), s32[]{:S(2)}) async-start(), calls=%async_computation.16 | async-start | bytes 5242880 | tf_op jit(solution)/shard_map/while/body/eval_jaxpr/reduce_scatter | solution.py:93
  666.7 206.8 %reduce-scatter.26.cloned.1.call-start = ((), (), s32[]{:S(2)}) async-start(), calls=%async_computation.17 | async-start | bytes 5242880 | tf_op jit(solution)/shard_map/while/body/eval_jaxpr/reduce_scatter | solution.py:93
  897.6 146.5 %reduce-scatter.28.cloned.1.call-start = ((), (), s32[]{:S(2)}) async-start(), calls=%async_computation.18 | async-start | bytes 5242880 | tf_op jit(solution)/shard_map/while/body/eval_jaxpr/reduce_scatter | solution.py:93
  967.5 207.5 %reduce-scatter.30.cloned.1.call-start = ((), (), s32[]{:S(2)}) async-start(), calls=%async_computation.19 | async-start | bytes 5242880 | tf_op jit(solution)/shard_map/while/body/eval_jaxpr/reduce_scatter | solution.py:93
  1099.0 128.4 %all-gather.3.cloned.1.call-start = ((), (), s32[]{:S(2)}) async-start(), calls=%async_computation.20 | async-start | bytes 2621440 | tf_op jit(solution)/shard_map/while/body/eval_jaxpr/all_gather | solution.py:106
  1180.8 136.0 %reduce-scatter.32.cloned.1.call-start = ((), (), s32[]{:S(2)}) async-start(), calls=%async_computation.21 | async-start | bytes 5242880 | tf_op jit(solution)/shard_map/while/body/eval_jaxpr/reduce_scatter | solution.py:114
  1321.6 160.6 %reduce-scatter.34.cloned.1.call-start = ((), (), s32[]{:S(2)}) async-start(), calls=%async_computation.23 | async-start | bytes 5242880 | tf_op jit(solution)/shard_map/while/body/eval_jaxpr/reduce_scatter | solution.py:114
  1502.7 144.6 %reduce-scatter.28.cloned.1.call-start = ((), (), s32[]{:S(2)}) async-start(), calls=%async_computation.18 | async-start | bytes 5242880 | tf_op jit(solution)/shard_map/while/body/eval_jaxpr/reduce_scatter | solution.py:93
  1572.6 205.7 %reduce-scatter.30.cloned.1.call-start = ((), (), s32[]{:S(2)}) async-start(), calls=%async_computation.19 | async-start | bytes 5242880 | tf_op jit(solution)/shard_map/while/body/eval_jaxpr/reduce_scatter | solution.py:93
  1702.2 128.4 %all-gather.3.cloned.1.call-start = ((), (), s32[]{:S(2)}) async-start(), calls=%async_computation.20 | async-start | bytes 2621440 | tf_op jit(solution)/shard_map/while/body/eval_jaxpr/all_gather | solution.py:106
  1784.0 135.9 %reduce-scatter.32.cloned.1.call-start = ((), (), s32[]{:S(2)}) async-start(), calls=%async_computation.21 | async-start | bytes 5242880 | tf_op jit(solution)/shard_map/while/body/eval_jaxpr/reduce_scatter | solution.py:114
  1844.3 127.1 %all-gather.5.cloned.1.call-start = ((), (), s32[]{:S(2)}) async-start(), calls=%async_computation.22 | async-start | bytes 2621440 | tf_op jit(solution)/shard_map/while/body/eval_jaxpr/all_gather | solution.py:106
  1924.8 160.8 %reduce-scatter.34.cloned.1.call-start = ((), (), s32[]{:S(2)}) async-start(), calls=%async_computation.23 | async-start | bytes 5242880 | tf_op jit(solution)/shard_map/while/body/eval_jaxpr/reduce_scatter | solution.py:114
  2106.0 144.6 %reduce-scatter.28.cloned.1.call-start = ((), (), s32[]{:S(2)}) async-start(), calls=%async_computation.18 | async-start | bytes 5242880 | tf_op jit(solution)/shard_map/while/body/eval_jaxpr/reduce_scatter | solution.py:93
  2175.8 205.7 %reduce-scatter.30.cloned.1.call-start = ((), (), s32[]{:S(2)}) async-start(), calls=%async_computation.19 | async-start | bytes 5242880 | tf_op jit(solution)/shard_map/while/body/eval_jaxpr/reduce_scatter | solution.py:93
  2305.5 128.4 %all-gather.3.cloned.1.call-start = ((), (), s32[]{:S(2)}) async-start(), calls=%async_computation.20 | async-start | bytes 2621440 | tf_op jit(solution)/shard_map/while/body/eval_jaxpr/all_gather | solution.py:106
  2387.3 135.9 %reduce-scatter.32.cloned.1.call-start = ((), (), s32[]{:S(2)}) async-start(), calls=%async_computation.21 | async-start | bytes 5242880 | tf_op jit(solution)/shard_map/while/body/eval_jaxpr/reduce_scatter | solution.py:114
  2528.1 160.6 %reduce-scatter.34.cloned.1.call-start = ((), (), s32[]{:S(2)}) async-start(), calls=%async_computation.23 | async-start | bytes 5242880 | tf_op jit(solution)/shard_map/while/body/eval_jaxpr/reduce_scatter | solution.py:114
  2718.4 141.1 %reduce-scatter.20.cloned.1.call-start = ((), (), s32[]{:S(2)}) async-start(), calls=%async_computation.14 | async-start | bytes 2621440 | tf_op jit(solution)/shard_map/reduce_scatter | solution.py:324
  2722.4 171.1 %reduce-scatter.18.cloned.1.call-start = ((), (), s32[]{:S(2)}) async-start(), calls=%async_computation.13 | async-start | bytes 2621440 | tf_op jit(solution)/shard_map/reduce_scatter | solution.py:321
  (184 other events, 4474.9 us)
Sparse Core Ops, SparseCore 0:
  84.2 76.0 reduce-scatter.23
  214.6 75.8 reduce-scatter.25
  375.4 76.4 reduce-scatter.23
  506.1 75.8 reduce-scatter.25
  666.9 76.4 reduce-scatter.23
  797.6 75.8 reduce-scatter.25
  967.6 76.4 reduce-scatter.27
  1099.1 75.8 reduce-scatter.29
  1180.9 46.4 all-gather.2
  1241.2 75.4 reduce-scatter.31
  1321.7 46.4 all-gather.4
  1406.6 75.4 reduce-scatter.33
  1572.7 74.5 reduce-scatter.27
  1702.3 75.9 reduce-scatter.29
  1784.1 46.4 all-gather.2
  1844.4 75.4 reduce-scatter.31
  1924.9 46.4 all-gather.4
  2010.1 75.4 reduce-scatter.33
  2175.9 74.5 reduce-scatter.27
  2305.6 75.9 reduce-scatter.29
  2387.4 46.4 all-gather.2
  2447.7 75.4 reduce-scatter.31
  2528.2 46.4 all-gather.4
  2613.1 75.4 reduce-scatter.33
Sparse Core Ops, SparseCore 1:
  2715.7 55.4 reduce-scatter.21
  2774.3 20.5 reduce-scatter.15
  2797.3 28.1 reduce-scatter.13
  2828.2 31.3 reduce-scatter.19
  2862.1 31.3 reduce-scatter.17
